TPU v7x, 512 devices: a whole 4x4x16 slice. The times are simulated.
512 devices in a mesh: head: 8 (over y, x_hi), seq: 16 (over z), dp: 4 (over x_lo, core).
Axes of the slice: x: 4 (x_hi: 2, x_lo: 2; x = x_hi * 2 + x_lo), y: 4, z: 16, core: 2. Of those that a mesh axis runs over, the one named last changes fastest.
Arguments:
- teacher_query: bfloat16 [4, 2048, 3072], P('dp', 'seq', 'head'), may hold values from -6 to 6
- teacher_key: bfloat16 [4, 2048, 3072], P('dp', 'seq', 'head'), may hold values from -6 to 6
- student_query: bfloat16 [4, 2048, 512], P('dp', 'seq'), may hold values from -6 to 6
- student_key: bfloat16 [4, 2048, 512], P('dp', 'seq'), may hold values from -6 to 6
- head_mix: float32 [24, 8], P('head'), may hold values from 0.02 to 0.25
Outputs:
- grad_query: float32 [4, 2048, 512], P('dp', 'seq', 'head')
- grad_key: float32 [4, 2048, 512], P('dp', 'seq', 'head')
- grad_mix: float32 [24, 8], P('head')
- head_loss: float32 [24], P('head')
All inputs are finite; a program needn't handle non-finite values.
Results may differ from a plain program's by a relative error of at most 0.0012.
Values may be sent and summed in bfloat16 or wider, within the bound.
A program may use at most 64 MiB of HBM per device.

v0:
```python
import math
import jax
import jax.numpy as jnp
from jax import lax
from jax.sharding import PartitionSpec as P

HEADS_T = 24
HD_T = 128
HEADS_S = 8
HD_S = 64


def from_behind(block, axis, distance):
    devices = range(lax.axis_size(axis))
    route = [((i - distance) % len(devices), i) for i in devices]
    return lax.ppermute(block, axis, route)


def lift_heads(head_mix, student):
    lifted = head_mix[:, 0, None, None] * student[0][None]
    for index in range(1, HEADS_S):
        lifted = lifted + head_mix[:, index, None, None] * student[index][None]
    return lifted


def block_maps(query_t, query_s, key_t, key_s, head_mix):
    row_count = query_t.shape[0]
    key_count = key_t.shape[0]
    teacher_heads = head_mix.shape[0]
    teacher = jnp.einsum(
        "rhd,khd->hrk",
        query_t.reshape(row_count, teacher_heads, HD_T),
        key_t.reshape(key_count, teacher_heads, HD_T),
        preferred_element_type=jnp.float32,
    ) * HD_T ** (-0.5)
    student = jnp.einsum(
        "rhd,khd->hrk",
        query_s.reshape(row_count, HEADS_S, HD_S),
        key_s.reshape(key_count, HEADS_S, HD_S),
        preferred_element_type=jnp.float32,
    ) * HD_S ** (-0.5)
    lifted = lift_heads(head_mix, student)
    return (teacher, student, lifted)


def absorb(stats, teacher, lifted):
    top_t, total_t, top_l, total_l = stats
    new_t = jnp.maximum(top_t, jnp.max(teacher, axis=-1))
    new_l = jnp.maximum(top_l, jnp.max(lifted, axis=-1))
    total_t = total_t * jnp.exp(top_t - new_t) + jnp.sum(
        jnp.exp(teacher - new_t[..., None]), axis=-1
    )
    total_l = total_l * jnp.exp(top_l - new_l) + jnp.sum(
        jnp.exp(lifted - new_l[..., None]), axis=-1
    )
    return (new_t, total_t, new_l, total_l)


def pair_terms(query_t, query_s, key_t, key_s, head_mix, lse_t, lse_l):
    teacher, student, lifted = block_maps(query_t, query_s, key_t, key_s, head_mix)
    prob_t = jnp.exp(teacher - lse_t[..., None])
    prob_l = jnp.exp(lifted - lse_l[..., None])
    kl_part = jnp.sum(prob_t * (teacher - lifted), axis=-1)
    excess = prob_l - prob_t
    mix_columns = []
    mixed_rows = []
    for index in range(HEADS_S):
        mix_columns.append(jnp.sum(excess * student[index][None], axis=(1, 2)))
        mixed_rows.append(jnp.sum(head_mix[:, index, None, None] * excess, axis=0))
    mix_part = jnp.stack(mix_columns, axis=1)
    mixed_grad = jnp.stack(mixed_rows, axis=0).astype(jnp.bfloat16)
    return (kl_part, mix_part, mixed_grad)


def query_side(mixed_grad, key_s):
    key_count = key_s.shape[0]
    result = jnp.einsum(
        "hrk,khd->rhd",
        mixed_grad,
        key_s.reshape(key_count, HEADS_S, HD_S),
        preferred_element_type=jnp.float32,
    )
    return result.reshape(result.shape[0], HEADS_S * HD_S)


def key_side(mixed_grad, query_s):
    row_count = query_s.shape[0]
    result = jnp.einsum(
        "hrk,rhd->khd",
        mixed_grad,
        query_s.reshape(row_count, HEADS_S, HD_S),
        preferred_element_type=jnp.float32,
    )
    return result.reshape(result.shape[0], HEADS_S * HD_S)


def body(teacher_query, teacher_key, student_query, student_key, head_mix):
    query_t = teacher_query[0]
    query_s = student_query[0]
    own_t = teacher_key[0]
    own_s = student_key[0]
    row_count = query_t.shape[0]
    teacher_heads = head_mix.shape[0]
    group_size = lax.axis_size("seq")
    position = lax.axis_index("seq")
    shards_per = math.gcd(group_size, max(1, 512 // row_count))
    block_rows = shards_per * row_count
    block_count = group_size // shards_per
    gathered = (
        lax.all_gather(teacher_key, "seq", axis=1, tiled=True),
        lax.all_gather(student_key, "seq", axis=1, tiled=True),
    )
    keys_t = gathered[0][0]
    keys_s = gathered[1][0]

    def first_pass(index, stats):
        start = index * block_rows
        key_t = lax.dynamic_slice_in_dim(keys_t, start, block_rows, 0)
        key_s = lax.dynamic_slice_in_dim(keys_s, start, block_rows, 0)
        teacher, student, lifted = block_maps(query_t, query_s, key_t, key_s, head_mix)
        return absorb(stats, teacher, lifted)

    floor_value = jnp.full((teacher_heads, row_count), -1e30, jnp.float32)
    zero_rows = jnp.zeros((teacher_heads, row_count), jnp.float32)
    stats = lax.fori_loop(
        0, block_count, first_pass, (floor_value, zero_rows, floor_value, zero_rows)
    )
    lse_t = stats[0] + jnp.log(stats[1])
    lse_l = stats[2] + jnp.log(stats[3])
    kl_sum, mix_sum, mixed_grad = pair_terms(query_t, query_s, own_t, own_s, head_mix, lse_t, lse_l)
    query_grad = query_side(mixed_grad, own_s)
    carried = key_side(mixed_grad, query_s)

    def second_pass(turn, carry):
        kl_acc, mix_acc, query_acc, moving = carry
        moving = from_behind(moving, "seq", 1)
        start = (position - turn) % group_size * row_count
        key_t = lax.dynamic_slice_in_dim(keys_t, start, row_count, 0)
        key_s = lax.dynamic_slice_in_dim(keys_s, start, row_count, 0)
        kl_part, mix_part, mixed = pair_terms(
            query_t, query_s, key_t, key_s, head_mix, lse_t, lse_l
        )
        return (
            kl_acc + kl_part,
            mix_acc + mix_part,
            query_acc + query_side(mixed, key_s),
            moving + key_side(mixed, query_s),
        )

    kl_sum, mix_sum, query_grad, carried = lax.fori_loop(
        1, group_size, second_pass, (kl_sum, mix_sum, query_grad, carried)
    )
    key_grad = from_behind(carried, "seq", 1)
    seq_len = row_count * group_size
    images = lax.axis_size("dp") * teacher_query.shape[0]
    weight = seq_len / HEADS_T
    factor = weight * HD_S ** (-0.5)
    grad_query, grad_key = (
        lax.psum_scatter((query_grad * factor)[None], "head", scatter_dimension=2, tiled=True),
        lax.psum_scatter((key_grad * factor)[None], "head", scatter_dimension=2, tiled=True),
    )
    kl_rows = jnp.sum(kl_sum - lse_t + lse_l, axis=-1)
    mix_total, loss_total = lax.psum((mix_sum, kl_rows), ("seq", "dp"))
    grad_mix = mix_total * (weight / (images * seq_len))
    head_loss = loss_total / (images * seq_len)
    return (grad_query, grad_key, grad_mix, head_loss)


def solution(mesh):
    return jax.shard_map(
        body,
        mesh=mesh,
        in_specs=(
            P("dp", "seq", "head"),
            P("dp", "seq", "head"),
            P("dp", "seq", None),
            P("dp", "seq", None),
            P("head", None),
        ),
        out_specs=(P("dp", "seq", "head"), P("dp", "seq", "head"), P("head", None), P("head")),
        check_vma=False,
    )
```

profile of v0, /device:TPU:32, one launch (start us, length us, event | category | flops | bytes accessed | tf_op | source)
XLA Modules:
  0.0 524.6 jit_solution(4273540421250965893)
XLA Ops:
  15.8 73.2 %all-gather.3.cloned.1.call-done = bf16[1,2048,384]{1,2,0:T(8,128)(2,1)} async-done(((bf16[1,128,384]{1,2,0:T(8,128)(2,1)}), bf16[1,2048,384]{1,2,0:T(8,128)(2,1)}) %all-gather.3.cloned.1.call-update) | async-done | bytes 1572880 | tf_op jit(solution)/shard_map/all_gather | solution.py:110
  89.1 76.4 %all-gather.5.cloned.1.call-done = bf16[1,2048,512]{1,2,0:T(8,128)(2,1)} async-done(((bf16[1,128,512]{1,2,0:T(8,128)(2,1)}), bf16[1,2048,512]{1,2,0:T(8,128)(2,1)}) %all-gather.5.cloned.1.call-update) | async-done | bytes 2097168 | tf_op jit(solution)/shard_map/all_gather | solution.py:111
  165.4 22.7 %while.42 = (s32[]{:T(128)}, f32[3,128]{1,0:T(4,128)S(1)}, f32[3,128]{1,0:T(4,128)S(1)}, f32[3,128]{1,0:T(4,128)S(1)}, f32[3,128]{1,0:T(4,128)S(1)}, /*index=5*/...) while((s32[]{:T(128)}, f32[3,128]{1,0:T(4,128)S(1)}, ...), condition=%wide.region_5.0_spmd.clone, body=%wide.region_0.0_spmd.clone.sunk | while | flops 125243136 | bytes 19275332 | solution.py:125
  190.6 155.4 %while.41 = (s32[]{:T(128)}, f32[3,128]{1,0:T(4,128)S(1)}, f32[3,8]{0,1:T(8,128)S(1)}, f32[128,512]{0,1:T(8,128)S(1)}, f32[128,512]{0,1:T(8,128)S(1)}, /*index=5...) while((s32[]{:T(128)}, f32[3,128]{1,0:T(4,128)S(1)}, ...), condition=%wide.region_41.42_spmd, body=%wide.region_23.41_spmd.sunk | while | flops 66486288 | bytes 9580356 | solution.py:150
  190.6 2.9 collective-permute-start
  198.9 2.9 collective-permute-start
  207.9 2.2 collective-permute-start
  214.7 4.1 collective-permute-done
  225.4 5.6 %collective-permute-done = f32[128,512]{0,1:T(8,128)S(1)} collective-permute-done((f32[128,512]{0,1:T(8,128)S(1)}, f32[128,512]{0,1:T(8,128)S(1)}, u32[]{:S(2)}, u32[]{:S(2)}) %collective-permute-start) | collective-permute-done | bytes 262176 | tf_op jit(solution)/shard_map/while/body/eval_jaxpr/ppermute | solution.py:16
  237.6 5.4 %collective-permute-done = f32[128,512]{0,1:T(8,128)S(1)} collective-permute-done((f32[128,512]{0,1:T(8,128)S(1)}, f32[128,512]{0,1:T(8,128)S(1)}, u32[]{:S(2)}, u32[]{:S(2)}) %collective-permute-start) | collective-permute-done | bytes 262176 | tf_op jit(solution)/shard_map/while/body/eval_jaxpr/ppermute | solution.py:16
  249.6 4.0 collective-permute-done
  260.2 3.2 collective-permute-done
  270.0 2.6 collective-permute-done
  279.2 2.9 collective-permute-done
  282.2 1.9 collective-permute-start
  288.8 2.9 collective-permute-done
  298.3 4.1 collective-permute-done
  309.0 5.4 %collective-permute-done = f32[128,512]{0,1:T(8,128)S(1)} collective-permute-done((f32[128,512]{0,1:T(8,128)S(1)}, f32[128,512]{0,1:T(8,128)S(1)}, u32[]{:S(2)}, u32[]{:S(2)}) %collective-permute-start) | collective-permute-done | bytes 262176 | tf_op jit(solution)/shard_map/while/body/eval_jaxpr/ppermute | solution.py:16
  320.9 5.7 %collective-permute-done = f32[128,512]{0,1:T(8,128)S(1)} collective-permute-done((f32[128,512]{0,1:T(8,128)S(1)}, f32[128,512]{0,1:T(8,128)S(1)}, u32[]{:S(2)}, u32[]{:S(2)}) %collective-permute-start) | collective-permute-done | bytes 262176 | tf_op jit(solution)/shard_map/while/body/eval_jaxpr/ppermute | solution.py:16
  333.3 3.2 collective-permute-done
  343.1 2.9 collective-permute-done
  348.8 7.5 %collective-permute-done.1 = f32[128,512]{0,1:T(8,128)S(1)} collective-permute-done((f32[128,512]{0,1:T(8,128)S(1)}, f32[128,512]{0,1:T(8,128)S(1)}, u32[]{:S(2)}, u32[]{:S(2)}) %collective-permute-start.1) | collective-permute-done | bytes 262176 | tf_op jit(solution)/shard_map/ppermute | solution.py:16
  357.2 100.6 %all-reduce = (f32[3,8]{1,0:T(4,128)S(1)}, f32[3]{0:T(128)S(1)}) all-reduce(f32[3,8]{1,0:T(4,128)S(1)} %copy.175, f32[3]{0:T(128)S(1)} %add_reduce_fusion), channel_id=1, replica_groups=mesh['head'=8,'seq'=16,'dp'=4] {'seq','dp'}, use_global_device_ids=true, to_apply=%region_44.45 | all-reduce | flops 27 | bytes 216 | tf_op jit(solution)/shard_map/psum | solution.py:163
  458.9 59.2 %reduce-scatter.5.cloned.1.call-done = f32[1,128,64]{1,2,0:T(8,128)} async-done(((f32[1,128,512]{1,2,0:T(8,128)}), f32[1,128,64]{1,2,0:T(8,128)}) %reduce-scatter.5.cloned.1.call-update) | async-done | bytes 32784 | tf_op jit(solution)/shard_map/reduce_scatter | solution.py:160
  (615 shorter events, 128.3 us)
Async XLA Ops:
  7.2 8.4 %copy-start.2 = (f32[3,8]{1,0:T(4,128)S(1)}, f32[3,8]{1,0:T(4,128)}, u32[]{:S(2)}) copy-start(f32[3,8]{1,0:T(4,128)} %param.13) | copy-start | bytes 292
  7.2 81.9 %all-gather.3.cloned.1.call-start = ((), (), s32[]{:S(2)}) async-start(), calls=%async_computation.2 | async-start | bytes 1671168 | tf_op jit(solution)/shard_map/all_gather | solution.py:110
  8.9 156.6 %all-gather.5.cloned.1.call-start = ((), (), s32[]{:S(2)}) async-start(), calls=%async_computation.3 | async-start | bytes 2228224 | tf_op jit(solution)/shard_map/all_gather | solution.py:111
  10.6 448.3 %reduce-scatter.3.cloned.1.call-start = ((), (), s32[]{:S(2)}) async-start(), calls=%async_computation.4 | async-start | bytes 294912 | tf_op jit(solution)/shard_map/reduce_scatter | solution.py:159
  165.4 22.8 %copy-start.1 = (bf16[1,128,384]{1,2,0:T(8,128)(2,1)S(1)}, bf16[1,128,384]{1,2,0:T(8,128)(2,1)}, u32[]{:S(2)}) copy-start(bf16[1,128,384]{1,2,0:T(8,128)(2,1)} %copy.146) | copy-start | bytes 294916
  188.2 2.1 copy-start
  190.6 8.3 %collective-permute-start = (f32[128,512]{0,1:T(8,128)S(1)}, f32[128,512]{0,1:T(8,128)S(1)}, u32[]{:S(2)}, u32[]{:S(2)}) collective-permute-start(f32[128,512]{0,1:T(8,128)S(1)} %get-tuple-element.1076), channel_id=1, source_target_pairs={{60,0},{0,4},{4,8},{8,12},{12,16},{16,20},{20,24},{24,28},{28,32},... | collective-permute-start | bytes 786440 | tf_op jit(solution)/shard_map/while/body/eval_jaxpr/ppermute | solution.py:16
  198.9 8.9 %collective-permute-start = (f32[128,512]{0,1:T(8,128)S(1)}, f32[128,512]{0,1:T(8,128)S(1)}, u32[]{:S(2)}, u32[]{:S(2)}) collective-permute-start(f32[128,512]{0,1:T(8,128)S(1)} %get-tuple-element.1076), channel_id=1, source_target_pairs={{60,0},{0,4},{4,8},{8,12},{12,16},{16,20},{20,24},{24,28},{28,32},... | collective-permute-start | bytes 786440 | tf_op jit(solution)/shard_map/while/body/eval_jaxpr/ppermute | solution.py:16
  207.9 11.0 %collective-permute-start = (f32[128,512]{0,1:T(8,128)S(1)}, f32[128,512]{0,1:T(8,128)S(1)}, u32[]{:S(2)}, u32[]{:S(2)}) collective-permute-start(f32[128,512]{0,1:T(8,128)S(1)} %get-tuple-element.1076), channel_id=1, source_target_pairs={{60,0},{0,4},{4,8},{8,12},{12,16},{16,20},{20,24},{24,28},{28,32},... | collective-permute-start | bytes 786440 | tf_op jit(solution)/shard_map/while/body/eval_jaxpr/ppermute | solution.py:16
  218.9 12.1 %collective-permute-start = (f32[128,512]{0,1:T(8,128)S(1)}, f32[128,512]{0,1:T(8,128)S(1)}, u32[]{:S(2)}, u32[]{:S(2)}) collective-permute-start(f32[128,512]{0,1:T(8,128)S(1)} %get-tuple-element.1076), channel_id=1, source_target_pairs={{60,0},{0,4},{4,8},{8,12},{12,16},{16,20},{20,24},{24,28},{28,32},... | collective-permute-start | bytes 786440 | tf_op jit(solution)/shard_map/while/body/eval_jaxpr/ppermute | solution.py:16
  231.0 12.0 %collective-permute-start = (f32[128,512]{0,1:T(8,128)S(1)}, f32[128,512]{0,1:T(8,128)S(1)}, u32[]{:S(2)}, u32[]{:S(2)}) collective-permute-start(f32[128,512]{0,1:T(8,128)S(1)} %get-tuple-element.1076), channel_id=1, source_target_pairs={{60,0},{0,4},{4,8},{8,12},{12,16},{16,20},{20,24},{24,28},{28,32},... | collective-permute-start | bytes 786440 | tf_op jit(solution)/shard_map/while/body/eval_jaxpr/ppermute | solution.py:16
  243.1 10.6 %collective-permute-start = (f32[128,512]{0,1:T(8,128)S(1)}, f32[128,512]{0,1:T(8,128)S(1)}, u32[]{:S(2)}, u32[]{:S(2)}) collective-permute-start(f32[128,512]{0,1:T(8,128)S(1)} %get-tuple-element.1076), channel_id=1, source_target_pairs={{60,0},{0,4},{4,8},{8,12},{12,16},{16,20},{20,24},{24,28},{28,32},... | collective-permute-start | bytes 786440 | tf_op jit(solution)/shard_map/while/body/eval_jaxpr/ppermute | solution.py:16
  253.7 9.7 %collective-permute-start = (f32[128,512]{0,1:T(8,128)S(1)}, f32[128,512]{0,1:T(8,128)S(1)}, u32[]{:S(2)}, u32[]{:S(2)}) collective-permute-start(f32[128,512]{0,1:T(8,128)S(1)} %get-tuple-element.1076), channel_id=1, source_target_pairs={{60,0},{0,4},{4,8},{8,12},{12,16},{16,20},{20,24},{24,28},{28,32},... | collective-permute-start | bytes 786440 | tf_op jit(solution)/shard_map/while/body/eval_jaxpr/ppermute | solution.py:16
  263.4 9.2 %collective-permute-start = (f32[128,512]{0,1:T(8,128)S(1)}, f32[128,512]{0,1:T(8,128)S(1)}, u32[]{:S(2)}, u32[]{:S(2)}) collective-permute-start(f32[128,512]{0,1:T(8,128)S(1)} %get-tuple-element.1076), channel_id=1, source_target_pairs={{60,0},{0,4},{4,8},{8,12},{12,16},{16,20},{20,24},{24,28},{28,32},... | collective-permute-start | bytes 786440 | tf_op jit(solution)/shard_map/while/body/eval_jaxpr/ppermute | solution.py:16
  272.7 9.5 %collective-permute-start = (f32[128,512]{0,1:T(8,128)S(1)}, f32[128,512]{0,1:T(8,128)S(1)}, u32[]{:S(2)}, u32[]{:S(2)}) collective-permute-start(f32[128,512]{0,1:T(8,128)S(1)} %get-tuple-element.1076), channel_id=1, source_target_pairs={{60,0},{0,4},{4,8},{8,12},{12,16},{16,20},{20,24},{24,28},{28,32},... | collective-permute-start | bytes 786440 | tf_op jit(solution)/shard_map/while/body/eval_jaxpr/ppermute | solution.py:16
  282.2 9.5 %collective-permute-start = (f32[128,512]{0,1:T(8,128)S(1)}, f32[128,512]{0,1:T(8,128)S(1)}, u32[]{:S(2)}, u32[]{:S(2)}) collective-permute-start(f32[128,512]{0,1:T(8,128)S(1)} %get-tuple-element.1076), channel_id=1, source_target_pairs={{60,0},{0,4},{4,8},{8,12},{12,16},{16,20},{20,24},{24,28},{28,32},... | collective-permute-start | bytes 786440 | tf_op jit(solution)/shard_map/while/body/eval_jaxpr/ppermute | solution.py:16
  291.7 10.7 %collective-permute-start = (f32[128,512]{0,1:T(8,128)S(1)}, f32[128,512]{0,1:T(8,128)S(1)}, u32[]{:S(2)}, u32[]{:S(2)}) collective-permute-start(f32[128,512]{0,1:T(8,128)S(1)} %get-tuple-element.1076), channel_id=1, source_target_pairs={{60,0},{0,4},{4,8},{8,12},{12,16},{16,20},{20,24},{24,28},{28,32},... | collective-permute-start | bytes 786440 | tf_op jit(solution)/shard_map/while/body/eval_jaxpr/ppermute | solution.py:16
  302.4 11.9 %collective-permute-start = (f32[128,512]{0,1:T(8,128)S(1)}, f32[128,512]{0,1:T(8,128)S(1)}, u32[]{:S(2)}, u32[]{:S(2)}) collective-permute-start(f32[128,512]{0,1:T(8,128)S(1)} %get-tuple-element.1076), channel_id=1, source_target_pairs={{60,0},{0,4},{4,8},{8,12},{12,16},{16,20},{20,24},{24,28},{28,32},... | collective-permute-start | bytes 786440 | tf_op jit(solution)/shard_map/while/body/eval_jaxpr/ppermute | solution.py:16
  314.4 12.3 %collective-permute-start = (f32[128,512]{0,1:T(8,128)S(1)}, f32[128,512]{0,1:T(8,128)S(1)}, u32[]{:S(2)}, u32[]{:S(2)}) collective-permute-start(f32[128,512]{0,1:T(8,128)S(1)} %get-tuple-element.1076), channel_id=1, source_target_pairs={{60,0},{0,4},{4,8},{8,12},{12,16},{16,20},{20,24},{24,28},{28,32},... | collective-permute-start | bytes 786440 | tf_op jit(solution)/shard_map/while/body/eval_jaxpr/ppermute | solution.py:16
  326.7 9.7 %collective-permute-start = (f32[128,512]{0,1:T(8,128)S(1)}, f32[128,512]{0,1:T(8,128)S(1)}, u32[]{:S(2)}, u32[]{:S(2)}) collective-permute-start(f32[128,512]{0,1:T(8,128)S(1)} %get-tuple-element.1076), channel_id=1, source_target_pairs={{60,0},{0,4},{4,8},{8,12},{12,16},{16,20},{20,24},{24,28},{28,32},... | collective-permute-start | bytes 786440 | tf_op jit(solution)/shard_map/while/body/eval_jaxpr/ppermute | solution.py:16
  336.5 9.5 %collective-permute-start = (f32[128,512]{0,1:T(8,128)S(1)}, f32[128,512]{0,1:T(8,128)S(1)}, u32[]{:S(2)}, u32[]{:S(2)}) collective-permute-start(f32[128,512]{0,1:T(8,128)S(1)} %get-tuple-element.1076), channel_id=1, source_target_pairs={{60,0},{0,4},{4,8},{8,12},{12,16},{16,20},{20,24},{24,28},{28,32},... | collective-permute-start | bytes 786440 | tf_op jit(solution)/shard_map/while/body/eval_jaxpr/ppermute | solution.py:16
  346.8 171.3 %reduce-scatter.5.cloned.1.call-start = ((), (), s32[]{:S(2)}) async-start(), calls=%async_computation.5 | async-start | bytes 294912 | tf_op jit(solution)/shard_map/reduce_scatter | solution.py:160
  346.8 9.5 %collective-permute-start.1 = (f32[128,512]{0,1:T(8,128)S(1)}, f32[128,512]{0,1:T(8,128)S(1)}, u32[]{:S(2)}, u32[]{:S(2)}) collective-permute-start(f32[128,512]{0,1:T(8,128)S(1)} %get-tuple-element.493), channel_id=1, source_target_pairs={{60,0},{0,4},{4,8},{8,12},{12,16},{16,20},{20,24},{24,28},{28,32},... | collective-permute-start | bytes 786440 | tf_op jit(solution)/shard_map/ppermute | solution.py:16
Sparse Core Ops, SparseCore 0:
  10.0 79.0 all-gather.2
  91.1 74.3 all-gather.4
  346.9 81.1 reduce-scatter.2
  432.9 85.1 reduce-scatter.4
where the time goes:
time: 526 us; the launch traced here: 525 us
  waiting for transfers between devices  270 us (51%)
  blocking collectives  101 us (19%)
  local copies, waits for them, and re-layouts  65.5 us (12%)
  starting transfers between devices  33.2 us (6%)
  matrix products  20.9 us (4%)
  other arithmetic  16.5 us (3%)
  between operations  14.1 us (3%)
    psum x1, blocking collectives, body(): mix_total, loss_total = lax.psum((mix_sum, kl_rows), ('seq', 'dp'))  101 us
    all_gather x1, waiting for transfers between devices, body(): lax.all_gather(student_key, 'seq', axis=1, tiled=True)  76.4 us
    all_gather x1, waiting for transfers between devices, body(): lax.all_gather(teacher_key, 'seq', axis=1, tiled=True)  73.2 us
    ppermute x16, waiting for transfers between devices, from_behind(): return lax.ppermute(block, axis, route)  61.6 us
    reduce_scatter x1, waiting for transfers between devices, body(): lax.psum_scatter((key_grad * factor)[None], 'head', scatter_dimension=2,...  59.2 us
    ppermute x16, starting transfers between devices, from_behind(): return lax.ppermute(block, axis, route)  33 us
    reduce_sum x128, local copies, waits for them, and re-layouts, pair_terms(): mixed_rows.append(jnp.sum(head_mix[:, index, None, None] * excess, axis=0))  15.2 us
    dynamic_slice x15, local copies, waits for them, and re-layouts, second_pass(): key_s = lax.dynamic_slice_in_dim(keys_s, start, row_count, 0)  13.8 us
  transfers between devices with their start and end apart: 20, of which 19 were waited for; matrix products, arithmetic and copies ran while one was open for 14% of the time, Pallas kernels for 0%

commit v1 on v0

--- a/solution.py
+++ b/solution.py
@@ -8,6 +8,22 @@
 HD_T = 128
 HEADS_S = 8
 HD_S = 64
+
+
+def gather_around(x, axis, dim):
+    ways, here, step = (lax.axis_size(axis), lax.axis_index(axis), x.shape[dim])
+    dims = [n * ways if d == dim else n for d, n in enumerate(x.shape)]
+    full = lax.dynamic_update_slice_in_dim(jnp.zeros(dims, x.dtype), x, here * step, axis=dim)
+    going_up = going_down = x
+    for far in range(1, ways // 2 + 1):
+        going_up = lax.ppermute(going_up, axis, [(d, (d + 1) % ways) for d in range(ways)])
+        full = lax.dynamic_update_slice_in_dim(full, going_up, (here - far) % ways * step, axis=dim)
+        if 2 * far < ways:
+            going_down = lax.ppermute(going_down, axis, [(d, (d - 1) % ways) for d in range(ways)])
+            full = lax.dynamic_update_slice_in_dim(
+                full, going_down, (here + far) % ways * step, axis=dim
+            )
+    return full
 
 
 def from_behind(block, axis, distance):
@@ -108,7 +124,7 @@
     block_count = group_size // shards_per
     gathered = (
         lax.all_gather(teacher_key, "seq", axis=1, tiled=True),
-        lax.all_gather(student_key, "seq", axis=1, tiled=True),
+        gather_around(student_key, "seq", 1),
     )
     keys_t = gathered[0][0]
     keys_s = gathered[1][0]

time: 526 us -> 456 us (0.87)
  waiting for transfers between devices: 270 us -> 136 us
  starting transfers between devices: 33.2 us -> 87.7 us
  local copies, waits for them, and re-layouts: 65.5 us -> 75.8 us
    all_gather x1 -> x0, waiting for transfers between devices: 76.4 us -> none  [body(): lax.all_gather(student_key, 'seq', axis=1, tiled=True)]
    all_gather x1, waiting for transfers between devices: 73.2 us -> 12.6 us  [body(): lax.all_gather(teacher_key, 'seq', axis=1, tiled=True)]
    ppermute x0 -> x15, starting transfers between devices: none -> 53.6 us  [the longest x7 36.4 us: gather_around(): lax.ppermute(going_down, axis, [(d, (d - 1) % ways) for d in range(ways)])]
    dynamic_update_slice x0 -> x16, local copies, waits for them, and re-layouts: none -> 10.9 us  [the longest x8 5.47 us: gather_around(): lax.dynamic_update_slice_in_dim(full, going_up, (here - far) % ways * ste...]
    ppermute x0 -> x15, waiting for transfers between devices: none -> 7.29 us  [the longest x8 7.22 us: gather_around(): lax.ppermute(going_up, axis, [(d, (d + 1) % ways) for d in range(ways)])]
    ppermute x16, waiting for transfers between devices: 61.6 us -> 55.4 us  [from_behind(): return lax.ppermute(block, axis, route)]
  transfers between devices with their start and end apart: 20 -> 34, of which waited for: 19 -> 24; matrix products, arithmetic and copies ran while one was open for 14% -> 19% of each run, Pallas kernels for 0% -> 0%
where the time goes in v1:
time: 456 us; the launch traced here: 454 us
  waiting for transfers between devices  136 us (30%)
  blocking collectives  101 us (22%)
  starting transfers between devices  87.7 us (19%)
  local copies, waits for them, and re-layouts  75.8 us (17%)
  matrix products  20 us (4%)
  other arithmetic  16.5 us (4%)
  between operations  14.3 us (3%)
    psum x1, blocking collectives, body(): mix_total, loss_total = lax.psum((mix_sum, kl_rows), ('seq', 'dp'))  101 us
    reduce_scatter x1, waiting for transfers between devices, body(): lax.psum_scatter((key_grad * factor)[None], 'head', scatter_dimension=2,...  60.8 us
    ppermute x16, waiting for transfers between devices, from_behind(): return lax.ppermute(block, axis, route)  55.4 us
    ppermute x7, starting transfers between devices, gather_around(): lax.ppermute(going_down, axis, [(d, (d - 1) % ways) for d in range(ways)])  36.4 us
    ppermute x16, starting transfers between devices, from_behind(): return lax.ppermute(block, axis, route)  33.9 us
    ppermute x8, starting transfers between devices, gather_around(): lax.ppermute(going_up, axis, [(d, (d + 1) % ways) for d in range(ways)])  17.2 us
    reduce_sum x128, local copies, waits for them, and re-layouts, pair_terms(): mixed_rows.append(jnp.sum(head_mix[:, index, None, None] * excess, axis=0))  15.2 us
    dynamic_slice x15, local copies, waits for them, and re-layouts, second_pass(): key_s = lax.dynamic_slice_in_dim(keys_s, start, row_count, 0)  13.8 us
  transfers between devices with their start and end apart: 34, of which 24 were waited for; matrix products, arithmetic and copies ran while one was open for 19% of the time, Pallas kernels for 0%

profile of v1, /device:TPU:32, one launch (start us, length us, event | category | flops | bytes accessed | tf_op | source)
XLA Modules:
  0.0 454.3 jit_solution(8675046888580790079)
XLA Ops:
  8.2 3.8 collective-permute-start.1
  12.1 5.5 %collective-permute-start.2 = (bf16[1,128,512]{1,2,0:T(8,128)(2,1)S(1)}, bf16[1,128,512]{1,2,0:T(8,128)(2,1)S(1)}, u32[]{:S(2)}, u32[]{:S(2)}) collective-permute-start(bf16[1,128,512]{1,2,0:T(8,128)(2,1)S(1)} %copy.156), channel_id=1, source_target_pairs={{0,60},{4,0},{8,4},{12,8},{16,12},{20,16},{24,20},{28,24},{32,28},... | collective-permute-start | bytes 393224 | tf_op jit(solution)/shard_map/ppermute | solution.py:22
  26.3 6.0 %collective-permute-start.4 = (bf16[1,128,512]{1,2,0:T(8,128)(2,1)S(1)}, bf16[1,128,512]{1,2,0:T(8,128)(2,1)S(1)}, u32[]{:S(2)}, u32[]{:S(2)}) collective-permute-start(bf16[1,128,512]{1,2,0:T(8,128)(2,1)S(1)} %collective-permute-done.2), channel_id=1, source_target_pairs={{0,60},{4,0},{8,4},{12,8},{16,12},{20,16},{24,20},{28,24},{32,28},... | collective-permute-start | bytes 393224 | tf_op jit(solution)/shard_map/ppermute | solution.py:22
  35.6 5.2 %collective-permute-start.6 = (bf16[1,128,512]{1,2,0:T(8,128)(2,1)S(1)}, bf16[1,128,512]{1,2,0:T(8,128)(2,1)S(1)}, u32[]{:S(2)}, u32[]{:S(2)}) collective-permute-start(bf16[1,128,512]{1,2,0:T(8,128)(2,1)S(1)} %collective-permute-done.4), channel_id=1, source_target_pairs={{0,60},{4,0},{8,4},{12,8},{16,12},{20,16},{24,20},{28,24},{32,28},... | collective-permute-start | bytes 393224 | tf_op jit(solution)/shard_map/ppermute | solution.py:22
  44.1 5.2 %collective-permute-start.8 = (bf16[1,128,512]{1,2,0:T(8,128)(2,1)S(1)}, bf16[1,128,512]{1,2,0:T(8,128)(2,1)S(1)}, u32[]{:S(2)}, u32[]{:S(2)}) collective-permute-start(bf16[1,128,512]{1,2,0:T(8,128)(2,1)S(1)} %collective-permute-done.6), channel_id=1, source_target_pairs={{0,60},{4,0},{8,4},{12,8},{16,12},{20,16},{24,20},{28,24},{32,28},... | collective-permute-start | bytes 393224 | tf_op jit(solution)/shard_map/ppermute | solution.py:22
  53.4 4.6 %collective-permute-start.10 = (bf16[1,128,512]{1,2,0:T(8,128)(2,1)S(1)}, bf16[1,128,512]{1,2,0:T(8,128)(2,1)S(1)}, u32[]{:S(2)}, u32[]{:S(2)}) collective-permute-start(bf16[1,128,512]{1,2,0:T(8,128)(2,1)S(1)} %collective-permute-done.8), channel_id=1, source_target_pairs={{0,60},{4,0},{8,4},{12,8},{16,12},{20,16},{24,20},{28,24},{32,28},... | collective-permute-start | bytes 393224 | tf_op jit(solution)/shard_map/ppermute | solution.py:22
  62.0 4.8 %collective-permute-start.12 = (bf16[1,128,512]{1,2,0:T(8,128)(2,1)S(1)}, bf16[1,128,512]{1,2,0:T(8,128)(2,1)S(1)}, u32[]{:S(2)}, u32[]{:S(2)}) collective-permute-start(bf16[1,128,512]{1,2,0:T(8,128)(2,1)S(1)} %collective-permute-done.10), channel_id=1, source_target_pairs={{0,60},{4,0},{8,4},{12,8},{16,12},{20,16},{24,20},{28,24},{32,28},... | collective-permute-start | bytes 393224 | tf_op jit(solution)/shard_map/ppermute | solution.py:22
  70.3 5.2 %collective-permute-start.14 = (bf16[1,128,512]{1,2,0:T(8,128)(2,1)S(1)}, bf16[1,128,512]{1,2,0:T(8,128)(2,1)S(1)}, u32[]{:S(2)}, u32[]{:S(2)}) collective-permute-start(bf16[1,128,512]{1,2,0:T(8,128)(2,1)S(1)} %collective-permute-done.12), channel_id=1, source_target_pairs={{0,60},{4,0},{8,4},{12,8},{16,12},{20,16},{24,20},{28,24},{32,28},... | collective-permute-start | bytes 393224 | tf_op jit(solution)/shard_map/ppermute | solution.py:22
  80.2 5.4 %collective-permute-done.15 = bf16[1,128,512]{1,2,0:T(8,128)(2,1)S(1)} collective-permute-done((bf16[1,128,512]{1,2,0:T(8,128)(2,1)S(1)}, bf16[1,128,512]{1,2,0:T(8,128)(2,1)S(1)}, u32[]{:S(2)}, u32[]{:S(2)}) %collective-permute-start.15) | collective-permute-done | bytes 131104 | tf_op jit(solution)/shard_map/ppermute | solution.py:19
  86.3 12.6 %all-gather.2.cloned.1.call-done = bf16[1,2048,384]{1,2,0:T(8,128)(2,1)} async-done(((bf16[1,128,384]{1,2,0:T(8,128)(2,1)}), bf16[1,2048,384]{1,2,0:T(8,128)(2,1)}) %all-gather.2.cloned.1.call-update) | async-done | bytes 1572880 | tf_op jit(solution)/shard_map/all_gather | solution.py:126
  98.9 22.7 %while.42 = (s32[]{:T(128)}, f32[3,128]{1,0:T(4,128)S(1)}, f32[3,128]{1,0:T(4,128)S(1)}, f32[3,128]{1,0:T(4,128)S(1)}, f32[3,128]{1,0:T(4,128)S(1)}, /*index=5*/...) while((s32[]{:T(128)}, f32[3,128]{1,0:T(4,128)S(1)}, ...), condition=%wide.region_5.6_spmd.clone, body=%wide.region_0.5_spmd.clone.sunk | while | flops 125243136 | bytes 19275332 | solution.py:141
  124.0 150.1 %while.41 = (s32[]{:T(128)}, f32[3,128]{1,0:T(4,128)S(1)}, f32[3,8]{0,1:T(8,128)S(1)}, f32[128,512]{0,1:T(8,128)S(1)}, f32[128,512]{0,1:T(8,128)S(1)}, /*index=5...) while((s32[]{:T(128)}, f32[3,128]{1,0:T(4,128)S(1)}, ...), condition=%wide.region_41.42_spmd, body=%wide.region_23.41_spmd.sunk | while | flops 66486288 | bytes 9580356 | solution.py:166
  132.3 2.9 collective-permute-start
  156.7 3.7 collective-permute-done
  166.9 5.2 %collective-permute-done = f32[128,512]{0,1:T(8,128)S(1)} collective-permute-done((f32[128,512]{0,1:T(8,128)S(1)}, f32[128,512]{0,1:T(8,128)S(1)}, u32[]{:S(2)}, u32[]{:S(2)}) %collective-permute-start) | collective-permute-done | bytes 262176 | tf_op jit(solution)/shard_map/while/body/eval_jaxpr/ppermute | solution.py:32
  178.7 5.7 %collective-permute-done = f32[128,512]{0,1:T(8,128)S(1)} collective-permute-done((f32[128,512]{0,1:T(8,128)S(1)}, f32[128,512]{0,1:T(8,128)S(1)}, u32[]{:S(2)}, u32[]{:S(2)}) %collective-permute-start) | collective-permute-done | bytes 262176 | tf_op jit(solution)/shard_map/while/body/eval_jaxpr/ppermute | solution.py:32
  191.0 4.3 collective-permute-done
  201.9 3.4 collective-permute-done
  240.2 3.6 collective-permute-done
  250.5 4.3 collective-permute-done
  261.4 3.2 collective-permute-done
  276.9 7.5 %collective-permute-done.16 = f32[128,512]{0,1:T(8,128)S(1)} collective-permute-done((f32[128,512]{0,1:T(8,128)S(1)}, f32[128,512]{0,1:T(8,128)S(1)}, u32[]{:S(2)}, u32[]{:S(2)}) %collective-permute-start.16) | collective-permute-done | bytes 262176 | tf_op jit(solution)/shard_map/ppermute | solution.py:32
  285.3 100.6 %all-reduce = (f32[3,8]{1,0:T(4,128)S(1)}, f32[3]{0:T(128)S(1)}) all-reduce(f32[3,8]{1,0:T(4,128)S(1)} %copy.183, f32[3]{0:T(128)S(1)} %add_reduce_fusion), channel_id=1, replica_groups=mesh['head'=8,'seq'=16,'dp'=4] {'seq','dp'}, use_global_device_ids=true, to_apply=%region_44.45 | all-reduce | flops 27 | bytes 216 | tf_op jit(solution)/shard_map/psum | solution.py:179
  387.0 60.8 %reduce-scatter.5.cloned.1.call-done = f32[1,128,64]{1,2,0:T(8,128)} async-done(((f32[1,128,512]{1,2,0:T(8,128)}), f32[1,128,64]{1,2,0:T(8,128)}) %reduce-scatter.5.cloned.1.call-update) | async-done | bytes 32784 | tf_op jit(solution)/shard_map/reduce_scatter | solution.py:176
  (659 shorter events, 173.2 us)
Async XLA Ops:
  7.2 91.7 %all-gather.2.cloned.1.call-start = ((), (), s32[]{:S(2)}) async-start(), calls=%async_computation.2 | async-start | bytes 1671168 | tf_op jit(solution)/shard_map/all_gather | solution.py:126
  8.2 16.1 %collective-permute-start.1 = (bf16[1,128,512]{1,2,0:T(8,128)(2,1)S(1)}, bf16[1,128,512]{1,2,0:T(8,128)(2,1)S(1)}, u32[]{:S(2)}, u32[]{:S(2)}) collective-permute-start(bf16[1,128,512]{1,2,0:T(8,128)(2,1)S(1)} %copy.156), channel_id=1, source_target_pairs={{0,4},{4,8},{8,12},{12,16},{16,20},{20,24},{24,28},{28,32},{32,36}... | collective-permute-start | bytes 393224 | tf_op jit(solution)/shard_map/ppermute | solution.py:19
  12.1 14.2 %collective-permute-start.2 = (bf16[1,128,512]{1,2,0:T(8,128)(2,1)S(1)}, bf16[1,128,512]{1,2,0:T(8,128)(2,1)S(1)}, u32[]{:S(2)}, u32[]{:S(2)}) collective-permute-start(bf16[1,128,512]{1,2,0:T(8,128)(2,1)S(1)} %copy.156), channel_id=1, source_target_pairs={{0,60},{4,0},{8,4},{12,8},{16,12},{20,16},{24,20},{28,24},{32,28},... | collective-permute-start | bytes 393224 | tf_op jit(solution)/shard_map/ppermute | solution.py:22
  19.2 367.8 %reduce-scatter.3.cloned.1.call-start = ((), (), s32[]{:S(2)}) async-start(), calls=%async_computation.3 | async-start | bytes 294912 | tf_op jit(solution)/shard_map/reduce_scatter | solution.py:175
  24.3 9.3 %collective-permute-start.3 = (bf16[1,128,512]{1,2,0:T(8,128)(2,1)S(1)}, bf16[1,128,512]{1,2,0:T(8,128)(2,1)S(1)}, u32[]{:S(2)}, u32[]{:S(2)}) collective-permute-start(bf16[1,128,512]{1,2,0:T(8,128)(2,1)S(1)} %collective-permute-done.1), channel_id=1, source_target_pairs={{0,4},{4,8},{8,12},{12,16},{16,20},{20,24},{24,28},{28,32},{32,36}... | collective-permute-start | bytes 393224 | tf_op jit(solution)/shard_map/ppermute | solution.py:19
  26.3 9.3 %collective-permute-start.4 = (bf16[1,128,512]{1,2,0:T(8,128)(2,1)S(1)}, bf16[1,128,512]{1,2,0:T(8,128)(2,1)S(1)}, u32[]{:S(2)}, u32[]{:S(2)}) collective-permute-start(bf16[1,128,512]{1,2,0:T(8,128)(2,1)S(1)} %collective-permute-done.2), channel_id=1, source_target_pairs={{0,60},{4,0},{8,4},{12,8},{16,12},{20,16},{24,20},{28,24},{32,28},... | collective-permute-start | bytes 393224 | tf_op jit(solution)/shard_map/ppermute | solution.py:22
  42.2 9.3 %collective-permute-start.7 = (bf16[1,128,512]{1,2,0:T(8,128)(2,1)S(1)}, bf16[1,128,512]{1,2,0:T(8,128)(2,1)S(1)}, u32[]{:S(2)}, u32[]{:S(2)}) collective-permute-start(bf16[1,128,512]{1,2,0:T(8,128)(2,1)S(1)} %collective-permute-done.5), channel_id=1, source_target_pairs={{0,4},{4,8},{8,12},{12,16},{16,20},{20,24},{24,28},{28,32},{32,36}... | collective-permute-start | bytes 393224 | tf_op jit(solution)/shard_map/ppermute | solution.py:19
  44.1 9.3 %collective-permute-start.8 = (bf16[1,128,512]{1,2,0:T(8,128)(2,1)S(1)}, bf16[1,128,512]{1,2,0:T(8,128)(2,1)S(1)}, u32[]{:S(2)}, u32[]{:S(2)}) collective-permute-start(bf16[1,128,512]{1,2,0:T(8,128)(2,1)S(1)} %collective-permute-done.6), channel_id=1, source_target_pairs={{0,60},{4,0},{8,4},{12,8},{16,12},{20,16},{24,20},{28,24},{32,28},... | collective-permute-start | bytes 393224 | tf_op jit(solution)/shard_map/ppermute | solution.py:22
  70.3 9.3 %collective-permute-start.14 = (bf16[1,128,512]{1,2,0:T(8,128)(2,1)S(1)}, bf16[1,128,512]{1,2,0:T(8,128)(2,1)S(1)}, u32[]{:S(2)}, u32[]{:S(2)}) collective-permute-start(bf16[1,128,512]{1,2,0:T(8,128)(2,1)S(1)} %collective-permute-done.12), channel_id=1, source_target_pairs={{0,60},{4,0},{8,4},{12,8},{16,12},{20,16},{24,20},{28,24},{32,28},... | collective-permute-start | bytes 393224 | tf_op jit(solution)/shard_map/ppermute | solution.py:22
  140.6 9.3 %collective-permute-start = (f32[128,512]{0,1:T(8,128)S(1)}, f32[128,512]{0,1:T(8,128)S(1)}, u32[]{:S(2)}, u32[]{:S(2)}) collective-permute-start(f32[128,512]{0,1:T(8,128)S(1)} %get-tuple-element.1076), channel_id=1, source_target_pairs={{60,0},{0,4},{4,8},{8,12},{12,16},{16,20},{20,24},{24,28},{28,32},... | collective-permute-start | bytes 786440 | tf_op jit(solution)/shard_map/while/body/eval_jaxpr/ppermute | solution.py:32
  150.0 10.3 %collective-permute-start = (f32[128,512]{0,1:T(8,128)S(1)}, f32[128,512]{0,1:T(8,128)S(1)}, u32[]{:S(2)}, u32[]{:S(2)}) collective-permute-start(f32[128,512]{0,1:T(8,128)S(1)} %get-tuple-element.1076), channel_id=1, source_target_pairs={{60,0},{0,4},{4,8},{8,12},{12,16},{16,20},{20,24},{24,28},{28,32},... | collective-permute-start | bytes 786440 | tf_op jit(solution)/shard_map/while/body/eval_jaxpr/ppermute | solution.py:32
  160.4 11.7 %collective-permute-start = (f32[128,512]{0,1:T(8,128)S(1)}, f32[128,512]{0,1:T(8,128)S(1)}, u32[]{:S(2)}, u32[]{:S(2)}) collective-permute-start(f32[128,512]{0,1:T(8,128)S(1)} %get-tuple-element.1076), channel_id=1, source_target_pairs={{60,0},{0,4},{4,8},{8,12},{12,16},{16,20},{20,24},{24,28},{28,32},... | collective-permute-start | bytes 786440 | tf_op jit(solution)/shard_map/while/body/eval_jaxpr/ppermute | solution.py:32
  172.2 12.2 %collective-permute-start = (f32[128,512]{0,1:T(8,128)S(1)}, f32[128,512]{0,1:T(8,128)S(1)}, u32[]{:S(2)}, u32[]{:S(2)}) collective-permute-start(f32[128,512]{0,1:T(8,128)S(1)} %get-tuple-element.1076), channel_id=1, source_target_pairs={{60,0},{0,4},{4,8},{8,12},{12,16},{16,20},{20,24},{24,28},{28,32},... | collective-permute-start | bytes 786440 | tf_op jit(solution)/shard_map/while/body/eval_jaxpr/ppermute | solution.py:32
  184.4 10.8 %collective-permute-start = (f32[128,512]{0,1:T(8,128)S(1)}, f32[128,512]{0,1:T(8,128)S(1)}, u32[]{:S(2)}, u32[]{:S(2)}) collective-permute-start(f32[128,512]{0,1:T(8,128)S(1)} %get-tuple-element.1076), channel_id=1, source_target_pairs={{60,0},{0,4},{4,8},{8,12},{12,16},{16,20},{20,24},{24,28},{28,32},... | collective-permute-start | bytes 786440 | tf_op jit(solution)/shard_map/while/body/eval_jaxpr/ppermute | solution.py:32
  195.3 10.0 %collective-permute-start = (f32[128,512]{0,1:T(8,128)S(1)}, f32[128,512]{0,1:T(8,128)S(1)}, u32[]{:S(2)}, u32[]{:S(2)}) collective-permute-start(f32[128,512]{0,1:T(8,128)S(1)} %get-tuple-element.1076), channel_id=1, source_target_pairs={{60,0},{0,4},{4,8},{8,12},{12,16},{16,20},{20,24},{24,28},{28,32},... | collective-permute-start | bytes 786440 | tf_op jit(solution)/shard_map/while/body/eval_jaxpr/ppermute | solution.py:32
  205.3 9.2 %collective-permute-start = (f32[128,512]{0,1:T(8,128)S(1)}, f32[128,512]{0,1:T(8,128)S(1)}, u32[]{:S(2)}, u32[]{:S(2)}) collective-permute-start(f32[128,512]{0,1:T(8,128)S(1)} %get-tuple-element.1076), channel_id=1, source_target_pairs={{60,0},{0,4},{4,8},{8,12},{12,16},{16,20},{20,24},{24,28},{28,32},... | collective-permute-start | bytes 786440 | tf_op jit(solution)/shard_map/while/body/eval_jaxpr/ppermute | solution.py:32
  214.6 9.5 %collective-permute-start = (f32[128,512]{0,1:T(8,128)S(1)}, f32[128,512]{0,1:T(8,128)S(1)}, u32[]{:S(2)}, u32[]{:S(2)}) collective-permute-start(f32[128,512]{0,1:T(8,128)S(1)} %get-tuple-element.1076), channel_id=1, source_target_pairs={{60,0},{0,4},{4,8},{8,12},{12,16},{16,20},{20,24},{24,28},{28,32},... | collective-permute-start | bytes 786440 | tf_op jit(solution)/shard_map/while/body/eval_jaxpr/ppermute | solution.py:32
  224.1 9.5 %collective-permute-start = (f32[128,512]{0,1:T(8,128)S(1)}, f32[128,512]{0,1:T(8,128)S(1)}, u32[]{:S(2)}, u32[]{:S(2)}) collective-permute-start(f32[128,512]{0,1:T(8,128)S(1)} %get-tuple-element.1076), channel_id=1, source_target_pairs={{60,0},{0,4},{4,8},{8,12},{12,16},{16,20},{20,24},{24,28},{28,32},... | collective-permute-start | bytes 786440 | tf_op jit(solution)/shard_map/while/body/eval_jaxpr/ppermute | solution.py:32
  233.6 10.2 %collective-permute-start = (f32[128,512]{0,1:T(8,128)S(1)}, f32[128,512]{0,1:T(8,128)S(1)}, u32[]{:S(2)}, u32[]{:S(2)}) collective-permute-start(f32[128,512]{0,1:T(8,128)S(1)} %get-tuple-element.1076), channel_id=1, source_target_pairs={{60,0},{0,4},{4,8},{8,12},{12,16},{16,20},{20,24},{24,28},{28,32},... | collective-permute-start | bytes 786440 | tf_op jit(solution)/shard_map/while/body/eval_jaxpr/ppermute | solution.py:32
  243.9 10.9 %collective-permute-start = (f32[128,512]{0,1:T(8,128)S(1)}, f32[128,512]{0,1:T(8,128)S(1)}, u32[]{:S(2)}, u32[]{:S(2)}) collective-permute-start(f32[128,512]{0,1:T(8,128)S(1)} %get-tuple-element.1076), channel_id=1, source_target_pairs={{60,0},{0,4},{4,8},{8,12},{12,16},{16,20},{20,24},{24,28},{28,32},... | collective-permute-start | bytes 786440 | tf_op jit(solution)/shard_map/while/body/eval_jaxpr/ppermute | solution.py:32
  254.8 9.8 %collective-permute-start = (f32[128,512]{0,1:T(8,128)S(1)}, f32[128,512]{0,1:T(8,128)S(1)}, u32[]{:S(2)}, u32[]{:S(2)}) collective-permute-start(f32[128,512]{0,1:T(8,128)S(1)} %get-tuple-element.1076), channel_id=1, source_target_pairs={{60,0},{0,4},{4,8},{8,12},{12,16},{16,20},{20,24},{24,28},{28,32},... | collective-permute-start | bytes 786440 | tf_op jit(solution)/shard_map/while/body/eval_jaxpr/ppermute | solution.py:32
  264.6 9.5 %collective-permute-start = (f32[128,512]{0,1:T(8,128)S(1)}, f32[128,512]{0,1:T(8,128)S(1)}, u32[]{:S(2)}, u32[]{:S(2)}) collective-permute-start(f32[128,512]{0,1:T(8,128)S(1)} %get-tuple-element.1076), channel_id=1, source_target_pairs={{60,0},{0,4},{4,8},{8,12},{12,16},{16,20},{20,24},{24,28},{28,32},... | collective-permute-start | bytes 786440 | tf_op jit(solution)/shard_map/while/body/eval_jaxpr/ppermute | solution.py:32
  274.9 172.9 %reduce-scatter.5.cloned.1.call-start = ((), (), s32[]{:S(2)}) async-start(), calls=%async_computation.4 | async-start | bytes 294912 | tf_op jit(solution)/shard_map/reduce_scatter | solution.py:176
  274.9 9.5 %collective-permute-start.16 = (f32[128,512]{0,1:T(8,128)S(1)}, f32[128,512]{0,1:T(8,128)S(1)}, u32[]{:S(2)}, u32[]{:S(2)}) collective-permute-start(f32[128,512]{0,1:T(8,128)S(1)} %get-tuple-element.493), channel_id=1, source_target_pairs={{60,0},{0,4},{4,8},{8,12},{12,16},{16,20},{20,24},{24,28},{28,32},... | collective-permute-start | bytes 786440 | tf_op jit(solution)/shard_map/ppermute | solution.py:32
  (13 other events, 112.1 us)
Sparse Core Ops, SparseCore 0:
  19.3 79.5 all-gather.1
  275.0 82.6 reduce-scatter.2
  362.6 85.1 reduce-scatter.4
